TPU v7x, 512 devices: a whole 4x4x16 slice. The times are simulated.
512 devices in a mesh: dp: 128 (over z, y, core), shard: 4 (over x).
Axes of the slice: x: 4, y: 4, z: 16, core: 2. Of those that a mesh axis runs over, the one named last changes fastest.
Arguments:
- key_grad: bfloat16 [128, 512, 2560], P('dp', 'shard'), may hold values from -90 to 90
- key_error: float32 [128, 512, 2560], P('dp', 'shard'), may hold values from -4 to 4
- router_grad: bfloat16 [128, 64, 2560], P('dp', 'shard'), may hold values from -90 to 90
- router_error: float32 [128, 64, 2560], P('dp', 'shard'), may hold values from -4 to 4
- norm_grad: bfloat16 [128, 2, 2560], P('dp', None, 'shard'), may hold values from -8 to 8
- key_basis: float32 [32, 2560], replicated, may hold values from -6 to 6
- router_basis: float32 [32, 2560], replicated, may hold values from -6 to 6
- key_momentum: float32 [512, 2560], P('shard', 'dp'), may hold values from -4 to 4
- key_weight: float32 [512, 2560], P('shard', 'dp'), may hold values from -4 to 4
- router_momentum: float32 [64, 2560], P('shard', 'dp'), may hold values from -4 to 4
- router_weight: float32 [64, 2560], P('shard', 'dp'), may hold values from -4 to 4
- norm_momentum: float32 [2, 2560], P(None, 'shard'), may hold values from -4 to 4
- norm_weight: float32 [2, 2560], P(None, 'shard'), may hold values from 0.5 to 1.5
Outputs:
- key_carry: float32 [128, 512, 2560], P('dp', 'shard')
- router_carry: float32 [128, 64, 2560], P('dp', 'shard')
- key_velocity: float32 [512, 2560], P('shard', 'dp')
- key_master: float32 [512, 2560], P('shard', 'dp')
- key_params: bfloat16 [512, 2560], P(None, 'dp')
- router_velocity: float32 [64, 2560], P('shard', 'dp')
- router_master: float32 [64, 2560], P('shard', 'dp')
- router_params: bfloat16 [64, 2560], P(None, 'dp')
- norm_velocity: float32 [2, 2560], P(None, 'shard')
- norm_master: float32 [2, 2560], P(None, 'shard')
- norm_params: bfloat16 [2, 2560], replicated
All inputs are finite; a program needn't handle non-finite values.
Results may differ from a plain program's by a relative error of at most 0.008.
Values may be sent and summed in bfloat16 or wider, within the bound.
No kernel may reach another device: no remote copies, remote signals or barrier semaphores. Data moves between devices by JAX's collectives and lax.ppermute only.
A program may use at most 64 MiB of HBM per device.

v0:
```python
import jax
import jax.numpy as jnp
from jax import lax
from jax.sharding import PartitionSpec as P

ROOT_STEPS = 4
highest = lax.Precision.HIGHEST
momentum_decay = 0.9
learning_rate = 0.1


def inverse_root(gram_matrix):
    scaling = jnp.sqrt(jnp.sum(gram_matrix * gram_matrix)) + 1e-06
    identity = jnp.eye(gram_matrix.shape[0], dtype=jnp.float32)
    square_side = gram_matrix / scaling
    root_side = identity
    for sweep_index in range(ROOT_STEPS):
        middle = 1.5 * identity - 0.5 * jnp.dot(root_side, square_side, precision=highest)
        square_side = jnp.dot(square_side, middle, precision=highest)
        root_side = jnp.dot(middle, root_side, precision=highest)
    return (root_side, scaling)


def project(old_basis, merged):
    return lax.dot_general(old_basis, merged, (((1,), (1,)), ((), ())), precision=highest)


def gram_of(factor_rows):
    return lax.dot_general(factor_rows, factor_rows, (((1,), (1,)), ((), ())), precision=highest)


def normalize(gram_matrix, factor_rows):
    root_side, scaling = inverse_root(gram_matrix)
    return jnp.dot(root_side, factor_rows, precision=highest) / jnp.sqrt(scaling)


def advance(momentum, weight, direction):
    velocity = momentum_decay * momentum + direction
    return (velocity, weight - learning_rate * velocity)


def body(
    key_grad,
    key_error,
    router_grad,
    router_error,
    norm_grad,
    key_basis,
    router_basis,
    key_momentum,
    key_weight,
    router_momentum,
    router_weight,
    norm_momentum,
    norm_weight,
):
    replicas = lax.axis_size("dp")
    rank_size = key_basis.shape[0]
    merged_key = key_grad[0].astype(jnp.float32) + key_error[0]
    merged_router = router_grad[0].astype(jnp.float32) + router_error[0]
    rows_key, rows_router, norm_sum = lax.psum(
        (
            project(key_basis, merged_key),
            project(router_basis, merged_router),
            norm_grad[0].astype(jnp.float32),
        ),
        "dp",
    )
    gram_key, gram_router = lax.psum((gram_of(rows_key), gram_of(rows_router)), "shard")
    ortho_key = normalize(gram_key, rows_key)
    ortho_router = normalize(gram_router, rows_router)
    key_part = lax.dot_general(merged_key, ortho_key, (((0,), (1,)), ((), ())), precision=highest)
    router_part = lax.dot_general(
        merged_router, ortho_router, (((0,), (1,)), ((), ())), precision=highest
    )
    column_sum = lax.psum(jnp.concatenate([key_part, router_part], axis=1), ("dp", "shard"))
    columns = column_sum / replicas
    approx_key = lax.dot_general(
        ortho_key, columns[:, :rank_size], (((0,), (1,)), ((), ())), precision=highest
    )
    approx_router = lax.dot_general(
        ortho_router, columns[:, rank_size:], (((0,), (1,)), ((), ())), precision=highest
    )
    col_width = key_momentum.shape[1]
    offset = lax.axis_index("dp") * col_width
    key_velocity, key_master = advance(
        key_momentum, key_weight, lax.dynamic_slice_in_dim(approx_key, offset, col_width, 1)
    )
    router_velocity, router_master = advance(
        router_momentum,
        router_weight,
        lax.dynamic_slice_in_dim(approx_router, offset, col_width, 1),
    )
    norm_velocity, norm_master = advance(norm_momentum, norm_weight, norm_sum / replicas)
    key_params, router_params, norm_params = (
        lax.all_gather(key_master.astype(jnp.bfloat16), "shard", axis=0, tiled=True),
        lax.all_gather(router_master.astype(jnp.bfloat16), "shard", axis=0, tiled=True),
        lax.all_gather(norm_master.astype(jnp.bfloat16), "shard", axis=1, tiled=True),
    )
    key_carry = (merged_key - approx_key)[None]
    router_carry = (merged_router - approx_router)[None]
    return (
        key_carry,
        router_carry,
        key_velocity,
        key_master,
        key_params,
        router_velocity,
        router_master,
        router_params,
        norm_velocity,
        norm_master,
        norm_params,
    )


def solution(mesh):
    return jax.shard_map(
        body,
        mesh=mesh,
        in_specs=(
            P("dp", "shard", None),
            P("dp", "shard", None),
            P("dp", "shard", None),
            P("dp", "shard", None),
            P("dp", None, "shard"),
            P(),
            P(),
            P("shard", "dp"),
            P("shard", "dp"),
            P("shard", "dp"),
            P("shard", "dp"),
            P(None, "shard"),
            P(None, "shard"),
        ),
        out_specs=(
            P("dp", "shard", None),
            P("dp", "shard", None),
            P("shard", "dp"),
            P("shard", "dp"),
            P(None, "dp"),
            P("shard", "dp"),
            P("shard", "dp"),
            P(None, "dp"),
            P(None, "shard"),
            P(None, "shard"),
            P(),
        ),
        check_vma=False,
    )
```

profile of v0, /device:TPU:8, one launch (start us, length us, event | category | flops | bytes accessed | tf_op | source)
XLA Modules:
  0.0 1036.4 jit_solution(1657459035492836335)
XLA Ops:
  7.2 0.7 bitcast_convert_fusion
  8.0 1.4 convolution_bitcast_fusion
  9.5 2.9 fusion.5
  12.4 497.1 %all-reduce = (f32[32,128]{1,0:T(8,128)S(1)}, f32[32,16]{0,1:T(8,128)S(1)}, f32[2,640]{1,0:T(2,128)S(1)}) all-reduce(f32[32,128]{1,0:T(8,128)S(1)} %fusion.5, f32[32,16]{0,1:T(8,128)S(1)} %convolution_bitcast_fusion, f32[2,640]{1,0:T(2,128)S(1)} %bitcast_convert_fusion), channel_id=1, replica_groups=mesh['dp'=128,'shard'=4] {'dp'}, use_global_device_ids=true, to_apply=%region_0.0 | all-reduce | flops 5888 | bytes 47104 | tf_op jit(solution)/shard_map/psum | solution.py:61
  509.6 0.2 fusion.37
  509.9 17.1 %all-reduce.1 = (f32[32,32]{1,0:T(8,128)S(1)}, f32[32,32]{1,0:T(8,128)S(1)}) all-reduce(f32[32,32]{1,0:T(8,128)S(1)} %fusion.31, f32[32,32]{1,0:T(8,128)S(1)} %fusion.37), channel_id=1, replica_groups=mesh['dp'=128,'shard'=4] {'shard'}, use_global_device_ids=true, to_apply=%region_1.0 | all-reduce | flops 2048 | bytes 16384 | tf_op jit(solution)/shard_map/psum | solution.py:69
  527.0 0.6 multiply_reduce_fusion
  528.7 0.2 fusion.10
  529.2 0.2 fusion.9
  531.3 0.2 fusion.13
  532.0 0.2 fusion.12
  532.3 0.2 convolution_divide_fusion
  532.5 0.9 fusion
  533.6 0.5 fusion.20
  534.1 0.9 pad_maximum_fusion
  535.0 0.6 fusion.28
  535.6 11.8 %all_gather.11 = bf16[2,2560]{1,0:T(2,128)(2,1)S(1)} all-gather(bf16[2,640]{1,0:T(2,128)(2,1)S(1)} %get-tuple-element.27), channel_id=1, replica_groups=mesh['dp'=128,'shard'=4] {'shard'}, dimensions={1}, use_global_device_ids=true | all-gather | bytes 12800 | tf_op jit(solution)/shard_map/all_gather | solution.py:98
  547.6 445.8 %all-reduce.4.cloned.1.call-done = f32[2560,64]{0,1:T(8,128)} async-done(((f32[2560,64]{0,1:T(8,128)}), f32[2560,64]{0,1:T(8,128)}) %all-reduce.4.cloned.1.call-update) | async-done | bytes 655376 | tf_op jit(solution)/shard_map/psum | solution.py:76
  993.4 1.1 broadcast_multiply_fusion
  994.6 0.3 fusion.16
  994.9 2.3 fusion.18
  997.2 0.7 fusion.23
  997.9 0.7 fusion.29
  998.6 12.0 %all_gather.10 = bf16[64,20]{1,0:T(8,128)(2,1)S(1)} all-gather(bf16[16,20]{1,0:T(8,128)(2,1)S(1)} %get-tuple-element.30), channel_id=1, replica_groups=mesh['dp'=128,'shard'=4] {'shard'}, dimensions={0}, use_global_device_ids=true | all-gather | bytes 3200 | tf_op jit(solution)/shard_map/all_gather | solution.py:97
  1010.6 0.7 copy.29
  1011.3 2.6 fusion.4
  1013.9 1.0 fusion.30
  1014.8 0.7 copy.27
  1015.5 0.7 copy.26
  1016.2 12.0 %all_gather.9 = bf16[512,20]{1,0:T(8,128)(2,1)S(1)} all-gather(bf16[128,20]{1,0:T(8,128)(2,1)S(1)} %get-tuple-element.33), channel_id=1, replica_groups=mesh['dp'=128,'shard'=4] {'shard'}, dimensions={0}, use_global_device_ids=true | all-gather | bytes 25600 | tf_op jit(solution)/shard_map/all_gather | solution.py:96
  1028.2 0.7 copy.28
  1028.9 0.6 copy.32
  (46 shorter events, 3.2 us)
Async XLA Ops:
  7.2 2.3 copy-start
  7.2 986.2 %all-reduce.4.cloned.1.call-start = ((), (), s32[]{:S(2)}) async-start(), calls=%async_computation | async-start | bytes 1310720 | tf_op jit(solution)/shard_map/psum | solution.py:76
  9.4 523.1 %copy-start.1 = (f32[1,128,2560]{2,1,0:T(8,128)S(1)}, f32[1,128,2560]{2,1,0:T(8,128)}, u32[]{:S(2)}) copy-start(f32[1,128,2560]{2,1,0:T(8,128)} %param.14) | copy-start | bytes 3932164
  9.5 523.1 %copy-start.2 = (bf16[1,128,2560]{2,1,0:T(8,128)(2,1)S(1)}, bf16[1,128,2560]{2,1,0:T(8,128)(2,1)}, u32[]{:S(2)}) copy-start(bf16[1,128,2560]{2,1,0:T(8,128)(2,1)} %param.13) | copy-start | bytes 1966084
  531.6 2.0 copy-start.3
  531.6 2.0 copy-start.4
  533.4 1.6 copy-start.9
  533.4 1.6 copy-start.10
  533.6 13.8 %copy-start.5 = (f32[128,20]{0,1:T(8,128)S(1)}, f32[128,20]{0,1:T(8,128)}, u32[]{:S(2)}) copy-start(f32[128,20]{0,1:T(8,128)} %param.20) | copy-start | bytes 30724
  533.6 13.9 %copy-start.6 = (f32[128,20]{0,1:T(8,128)S(1)}, f32[128,20]{0,1:T(8,128)}, u32[]{:S(2)}) copy-start(f32[128,20]{0,1:T(8,128)} %param.21) | copy-start | bytes 30724
  994.6 3.3 copy-start.7
  994.6 3.3 copy-start.8
Sparse Core Ops, SparseCore 0:
  535.1 458.2 all-reduce.3
where the time goes:
time: 1040 us
  blocking collectives  550 us (53%)
  waiting for transfers between devices  446 us (43%)
  between operations  15.8 us (2%)
  matrix products  12.1 us (1%)
    psum x1, blocking collectives, body(): lax.psum((project(key_basis, merged_key), project(router_basis, merged_ro...  497 us
    psum x1, waiting for transfers between devices, body(): lax.psum(jnp.concatenate([key_part, router_part], axis=1), ('dp', 'shard'))  446 us
  transfers between devices with their start and end apart: 1, of which 1 were waited for; matrix products, arithmetic and copies ran while one was open for 0% of the time, Pallas kernels for 0%

commit v1 on v0

--- a/solution.py
+++ b/solution.py
@@ -73,7 +73,7 @@
     router_part = lax.dot_general(
         merged_router, ortho_router, (((0,), (1,)), ((), ())), precision=highest
     )
-    column_sum = lax.psum(jnp.concatenate([key_part, router_part], axis=1), ("dp", "shard"))
+    column_sum = lax.psum(lax.psum(jnp.concatenate([key_part, router_part], axis=1), "dp"), "shard")
     columns = column_sum / replicas
     approx_key = lax.dot_general(
         ortho_key, columns[:, :rank_size], (((0,), (1,)), ((), ())), precision=highest

time: 1040 us -> 971 us (0.934)
  waiting for transfers between devices: 446 us -> 380 us
    psum x1 -> x2, waiting for transfers between devices: 446 us -> 380 us  [the longest x1 333 us: body(): lax.psum(jnp.concatenate([key_part, router_part], axis=1), 'dp')]
  transfers between devices with their start and end apart: 1 -> 2, of which waited for: 1 -> 2; matrix products, arithmetic and copies ran while one was open for 0% -> 0% of each run, Pallas kernels for 0% -> 0%
where the time goes in v1:
time: 971 us
  blocking collectives  550 us (57%)
  waiting for transfers between devices  380 us (39%)
  between operations  15.9 us (2%)
  matrix products  12.1 us (1%)
    psum x1, blocking collectives, body(): lax.psum((project(key_basis, merged_key), project(router_basis, merged_ro...  497 us
    psum x1, waiting for transfers between devices, body(): lax.psum(jnp.concatenate([key_part, router_part], axis=1), 'dp')  333 us
    psum x1, waiting for transfers between devices, body(): lax.psum(lax.psum(jnp.concatenate([key_part, router_part], axis=1), 'dp')...  47 us
  transfers between devices with their start and end apart: 2, of which 2 were waited for; matrix products, arithmetic and copies ran while one was open for 0% of the time, Pallas kernels for 0%

profile of v1, /device:TPU:8, one launch (start us, length us, event | category | flops | bytes accessed | tf_op | source)
XLA Modules:
  0.0 970.7 jit_solution(10527914500235261780)
XLA Ops:
  7.2 0.7 bitcast_convert_fusion
  8.0 1.4 convolution_bitcast_fusion
  9.5 2.9 fusion.5
  12.4 497.1 %all-reduce = (f32[32,128]{1,0:T(8,128)S(1)}, f32[32,16]{0,1:T(8,128)S(1)}, f32[2,640]{1,0:T(2,128)S(1)}) all-reduce(f32[32,128]{1,0:T(8,128)S(1)} %fusion.5, f32[32,16]{0,1:T(8,128)S(1)} %convolution_bitcast_fusion, f32[2,640]{1,0:T(2,128)S(1)} %bitcast_convert_fusion), channel_id=1, replica_groups=mesh['dp'=128,'shard'=4] {'dp'}, use_global_device_ids=true, to_apply=%region_0.0 | all-reduce | flops 5888 | bytes 47104 | tf_op jit(solution)/shard_map/psum | solution.py:61
  509.6 0.2 fusion.37
  509.9 17.1 %all-reduce.1 = (f32[32,32]{1,0:T(8,128)S(1)}, f32[32,32]{1,0:T(8,128)S(1)}) all-reduce(f32[32,32]{1,0:T(8,128)S(1)} %fusion.31, f32[32,32]{1,0:T(8,128)S(1)} %fusion.37), channel_id=1, replica_groups=mesh['dp'=128,'shard'=4] {'shard'}, use_global_device_ids=true, to_apply=%region_1.0 | all-reduce | flops 2048 | bytes 16384 | tf_op jit(solution)/shard_map/psum | solution.py:69
  527.0 0.6 multiply_reduce_fusion
  529.2 0.2 fusion.9
  531.3 0.2 fusion.13
  532.0 0.2 fusion.12
  532.3 0.2 convolution_divide_fusion
  532.5 0.9 fusion
  533.6 0.5 fusion.20
  534.1 0.9 pad_maximum_fusion
  535.1 332.9 %all-reduce.5.cloned.1.call-done = f32[2560,64]{0,1:T(8,128)} async-done(((f32[2560,64]{0,1:T(8,128)}), f32[2560,64]{0,1:T(8,128)}) %all-reduce.5.cloned.1.call-update) | async-done | bytes 655376 | tf_op jit(solution)/shard_map/psum | solution.py:76
  868.1 0.6 fusion.28
  868.7 12.1 %all_gather.11 = bf16[2,2560]{1,0:T(2,128)(2,1)S(1)} all-gather(bf16[2,640]{1,0:T(2,128)(2,1)S(1)} %get-tuple-element.27), channel_id=1, replica_groups=mesh['dp'=128,'shard'=4] {'shard'}, dimensions={1}, use_global_device_ids=true | all-gather | bytes 12800 | tf_op jit(solution)/shard_map/all_gather | solution.py:98
  880.9 47.0 %all-reduce.7.cloned.1.call-done = f32[2560,64]{0,1:T(8,128)} async-done(((f32[2560,64]{0,1:T(8,128)}), f32[2560,64]{0,1:T(8,128)}) %all-reduce.7.cloned.1.call-update) | async-done | bytes 655376 | tf_op jit(solution)/shard_map/psum | solution.py:76
  927.9 1.1 broadcast_multiply_fusion
  929.1 0.3 fusion.16
  929.4 2.3 fusion.18
  931.7 0.7 fusion.23
  932.4 0.7 fusion.29
  933.1 11.9 %all_gather.10 = bf16[64,20]{1,0:T(8,128)(2,1)S(1)} all-gather(bf16[16,20]{1,0:T(8,128)(2,1)S(1)} %get-tuple-element.30), channel_id=1, replica_groups=mesh['dp'=128,'shard'=4] {'shard'}, dimensions={0}, use_global_device_ids=true | all-gather | bytes 3200 | tf_op jit(solution)/shard_map/all_gather | solution.py:97
  945.0 0.7 copy.29
  945.7 2.6 fusion.4
  948.2 1.0 fusion.30
  949.2 0.7 copy.27
  949.9 0.7 copy.26
  950.6 12.0 %all_gather.9 = bf16[512,20]{1,0:T(8,128)(2,1)S(1)} all-gather(bf16[128,20]{1,0:T(8,128)(2,1)S(1)} %get-tuple-element.33), channel_id=1, replica_groups=mesh['dp'=128,'shard'=4] {'shard'}, dimensions={0}, use_global_device_ids=true | all-gather | bytes 25600 | tf_op jit(solution)/shard_map/all_gather | solution.py:96
  962.6 0.7 copy.28
  963.3 0.6 copy.33
  (49 shorter events, 3.4 us)
Async XLA Ops:
  7.2 2.3 copy-start
  7.2 860.8 %all-reduce.5.cloned.1.call-start = ((), (), s32[]{:S(2)}) async-start(), calls=%async_computation | async-start | bytes 1310720 | tf_op jit(solution)/shard_map/psum | solution.py:76
  9.4 523.1 %copy-start.1 = (f32[1,128,2560]{2,1,0:T(8,128)S(1)}, f32[1,128,2560]{2,1,0:T(8,128)}, u32[]{:S(2)}) copy-start(f32[1,128,2560]{2,1,0:T(8,128)} %param.14) | copy-start | bytes 3932164
  9.5 523.1 %copy-start.2 = (bf16[1,128,2560]{2,1,0:T(8,128)(2,1)S(1)}, bf16[1,128,2560]{2,1,0:T(8,128)(2,1)}, u32[]{:S(2)}) copy-start(bf16[1,128,2560]{2,1,0:T(8,128)(2,1)} %param.13) | copy-start | bytes 1966084
  531.6 2.0 copy-start.3
  531.6 2.0 copy-start.4
  534.1 334.0 %copy-start.9 = (f32[2,640]{1,0:T(2,128)S(1)}, f32[2,640]{1,0:T(2,128)}, u32[]{:S(2)}) copy-start(f32[2,640]{1,0:T(2,128)} %param.25) | copy-start | bytes 15364
  534.1 334.0 %copy-start.10 = (f32[2,640]{1,0:T(2,128)S(1)}, f32[2,640]{1,0:T(2,128)}, u32[]{:S(2)}) copy-start(f32[2,640]{1,0:T(2,128)} %param.24) | copy-start | bytes 15364
  534.1 346.6 %copy-start.5 = (f32[128,20]{0,1:T(8,128)S(1)}, f32[128,20]{0,1:T(8,128)}, u32[]{:S(2)}) copy-start(f32[128,20]{0,1:T(8,128)} %param.20) | copy-start | bytes 30724
  534.1 346.7 %copy-start.6 = (f32[128,20]{0,1:T(8,128)S(1)}, f32[128,20]{0,1:T(8,128)}, u32[]{:S(2)}) copy-start(f32[128,20]{0,1:T(8,128)} %param.21) | copy-start | bytes 30724
  535.0 392.9 %all-reduce.7.cloned.1.call-start = ((), (), s32[]{:S(2)}) async-start(), calls=%async_computation.1 | async-start | bytes 1310720 | tf_op jit(solution)/shard_map/psum | solution.py:76
  929.1 3.3 copy-start.7
  929.1 3.3 copy-start.8
Sparse Core Ops, SparseCore 0:
  535.1 332.8 all-reduce.4
  870.5 57.3 all-reduce.6
